TPU v7x, 256 devices: a whole 4x4x8 slice. The times are simulated.
256 devices in a mesh: req: 64 (over x, z, y_lo), kv: 4 (over y_hi, core).
Axes of the slice: x: 4, y: 4 (y_hi: 2, y_lo: 2; y = y_hi * 2 + y_lo), z: 8, core: 2. Of those that a mesh axis runs over, the one named last changes fastest.
Arguments:
- hidden: bfloat16 [64, 1024, 1536], P('req', 'kv'), may hold values from -6 to 6
- lengths: int32 [64], P('req'), may hold values from 1 to 2048, as said below
- key_cache: bfloat16 [64, 2048, 768], P('req', 'kv'), may hold values from -180 to 180
- value_cache: bfloat16 [64, 2048, 768], P('req', 'kv'), may hold values from -6 to 6
- norm_gain: bfloat16 [1536], replicated, may hold values from 0.099609375 to 1.8984375
- w_query: bfloat16 [1536, 1536], P('req', 'kv'), may hold values from -0.15625 to 0.15625
- w_key: bfloat16 [1536, 768], P('req', 'kv'), may hold values from -0.15625 to 0.15625
- w_value: bfloat16 [1536, 768], P('req', 'kv'), may hold values from -0.15625 to 0.15625
- w_out: bfloat16 [1536, 1536], P('req', 'kv'), may hold values from -0.15625 to 0.15625
Outputs:
- attended: bfloat16 [64, 1024, 1536], P('req', 'kv')
- new_keys: bfloat16 [64, 1024, 768], P('req', 'kv')
- new_values: bfloat16 [64, 1024, 768], P('req', 'kv')
Inputs may be any that keep to these rules, and one draw needn't show every extreme that they name: `lengths`: at least a quarter of the requests (one or more) hold more than 1792 tokens, one of them exactly 2048; the others hold fewer than 512.
All inputs are finite; a program needn't handle non-finite values.
Results may differ from a plain program's by a relative error of at most 0.011.
Values may be sent and summed in bfloat16 or wider, within the bound.
A program may use at most 192 MiB of HBM per device.

v0:
```python
import jax
import jax.numpy as jnp
from jax import lax
from jax.sharding import PartitionSpec as P

H = 16
KVH = 8
HD = 96
rope_base = 100000.0
masked_score = -1e30


def rms_norm(states, gain):
    mean_square = jnp.mean(states * states, axis=-1, keepdims=True)
    scaled = states * lax.rsqrt(mean_square + 1e-05) * gain.astype(jnp.float32)
    return scaled.astype(jnp.bfloat16)


def rotate(values, positions):
    count = values.shape[0]
    heads = values.shape[1] // HD
    half = HD // 2
    frequency = rope_base ** (-(jnp.arange(half, dtype=jnp.float32) * 2.0 / HD))
    angle = positions[:, None] * frequency[None, :]
    cosine = jnp.cos(angle)[:, None, :]
    sine = jnp.sin(angle)[:, None, :]
    shaped = values.reshape(count, heads, HD)
    first = shaped[..., :half]
    second = shaped[..., half:]
    turned = jnp.concatenate(
        [first * cosine - second * sine, second * cosine + first * sine], axis=-1
    )
    return turned.reshape(count, heads * HD)


def fold_three(inputs, pieces):
    return tuple((jnp.dot(inputs, piece, preferred_element_type=jnp.float32) for piece in pieces))


def fold_single(inputs, piece):
    return jnp.dot(inputs, piece, preferred_element_type=jnp.float32)


def combine_blocks(blocks, share):
    block_count = blocks.shape[0]
    count = blocks.shape[1]
    numerator = jnp.zeros((count, H, HD), jnp.float32)
    for block in range(block_count):
        weight_rows = jnp.transpose(share[block])[:, :, None]
        numerator = (
            numerator + blocks[block].reshape(count, H, HD).astype(jnp.float32) * weight_rows
        )
    denominator = jnp.transpose(jnp.sum(share, axis=0))[:, :, None]
    return (numerator / denominator).reshape(count, H * HD).astype(jnp.bfloat16)


def body(hidden, lengths, key_cache, value_cache, norm_gain, w_query, w_key, w_value, w_out):
    rows_here = hidden.shape[1]
    width = hidden.shape[2]
    kv_count = lax.axis_size("kv")
    kv_index = lax.axis_index("kv")
    appended = rows_here * kv_count
    slots = key_cache.shape[1]
    groups = H // KVH
    scale = HD ** (-0.5)
    length = lengths[0]
    normed = rms_norm(hidden[0].astype(jnp.float32), norm_gain)
    query_cols, key_cols, value_cols = (
        lax.all_gather(w_query, "kv", axis=1, tiled=True),
        lax.all_gather(w_key, "kv", axis=1, tiled=True),
        lax.all_gather(w_value, "kv", axis=1, tiled=True),
    )
    proj_query, proj_key, proj_value = fold_three(
        normed,
        (
            lax.all_gather(query_cols, "req", axis=0, tiled=True),
            lax.all_gather(key_cols, "req", axis=0, tiled=True),
            lax.all_gather(value_cols, "req", axis=0, tiled=True),
        ),
    )
    positions = (length + kv_index * rows_here + jnp.arange(rows_here, dtype=jnp.int32)).astype(
        jnp.float32
    )
    queries_here = rotate(proj_query, positions).astype(jnp.bfloat16)
    new_keys = rotate(proj_key, positions).astype(jnp.bfloat16)
    new_values = proj_value.astype(jnp.bfloat16)
    queries = lax.all_gather(queries_here, "kv", axis=0, tiled=True)
    keys_all = jnp.concatenate([key_cache[0], new_keys], axis=0)
    values_all = jnp.concatenate([value_cache[0], new_values], axis=0)
    key_count = keys_all.shape[0]
    query_index = jnp.arange(appended, dtype=jnp.int32)
    cache_live = kv_index * slots + jnp.arange(slots, dtype=jnp.int32) < length
    own_index = kv_index * rows_here + jnp.arange(rows_here, dtype=jnp.int32)
    visible = jnp.concatenate(
        [
            jnp.broadcast_to(cache_live[None, :], (appended, slots)),
            own_index[None, :] <= query_index[:, None],
        ],
        axis=1,
    )
    query_heads = jnp.transpose(queries.reshape(appended, KVH, groups, HD), (1, 0, 2, 3))
    key_heads = jnp.transpose(keys_all.reshape(key_count, KVH, HD), (1, 0, 2))
    value_heads = jnp.transpose(values_all.reshape(key_count, KVH, HD), (1, 0, 2))

    def attend(operands):
        query_block, key_block, value_block = operands
        score = (
            jnp.einsum("qgd,kd->gqk", query_block, key_block, preferred_element_type=jnp.float32)
            * scale
        )
        score = jnp.where(visible[None], score, masked_score)
        peak = jnp.max(score, axis=-1)
        weights = jnp.where(visible[None], jnp.exp(score - peak[..., None]), 0.0)
        total = jnp.sum(weights, axis=-1)
        context = jnp.einsum(
            "gqk,kd->qgd",
            weights.astype(jnp.bfloat16),
            value_block,
            preferred_element_type=jnp.float32,
        )
        divisor = jnp.transpose(jnp.maximum(total, 1.0))[:, :, None]
        return ((context / divisor).astype(jnp.bfloat16), peak, total)

    outputs, peaks, totals = lax.map(attend, (query_heads, key_heads, value_heads))
    block_output = jnp.transpose(outputs, (1, 0, 2, 3)).reshape(appended, width)
    peaks = peaks.reshape(H, appended)
    totals = totals.reshape(H, appended)
    peak_blocks, total_blocks = (
        lax.all_gather(peaks[None], "kv", axis=0, tiled=True),
        lax.all_gather(totals[None], "kv", axis=0, tiled=True),
    )
    peak_all = jnp.max(peak_blocks, axis=0)
    share = jnp.exp(peak_blocks - peak_all[None]) * total_blocks
    received = lax.all_to_all(block_output, "kv", split_axis=0, concat_axis=0, tiled=True)
    blocks_here = received.reshape(kv_count, rows_here, width)
    share_here = lax.dynamic_slice_in_dim(share, kv_index * rows_here, rows_here, 2)
    context_here = combine_blocks(blocks_here, share_here)
    out_cols = lax.all_gather(w_out, "kv", axis=1, tiled=True)
    result = fold_single(context_here, lax.all_gather(out_cols, "req", axis=0, tiled=True))
    return (result.astype(jnp.bfloat16)[None], new_keys[None], new_values[None])


def solution(mesh):
    return jax.shard_map(
        body,
        mesh=mesh,
        in_specs=(
            P("req", "kv", None),
            P("req"),
            P("req", "kv", None),
            P("req", "kv", None),
            P(),
            P("req", "kv"),
            P("req", "kv"),
            P("req", "kv"),
            P("req", "kv"),
        ),
        out_specs=(P("req", "kv", None), P("req", "kv", None), P("req", "kv", None)),
        check_vma=False,
    )
```

profile of v0, /device:TPU:16, one launch (start us, length us, event | category | flops | bytes accessed | tf_op | source)
XLA Modules:
  0.0 1278.3 jit_solution(5281821043887652498)
XLA Ops:
  7.2 7.5 all_gather.37
  14.8 7.0 all-gather.1
  22.6 6.9 all-gather
  31.7 1.4 fusion.36
  33.4 290.6 %all-gather.12.cloned.1.call-done = bf16[1536,1536]{1,0:T(8,128)(2,1)} async-done(((bf16[24,1536]{1,0:T(8,128)(2,1)}), bf16[1536,1536]{1,0:T(8,128)(2,1)}) %all-gather.12.cloned.1.call-update) | async-done | bytes 4718608 | tf_op jit(solution)/shard_map/all_gather | solution.py:76
  323.9 6.8 copy.49
  330.7 3.9 fusion.50
  335.9 7.5 all_gather.42
  344.7 279.0 %all-gather.10.cloned.1.call-done = bf16[1536,768]{1,0:T(8,128)(2,1)} async-done(((bf16[24,768]{1,0:T(8,128)(2,1)}), bf16[1536,768]{1,0:T(8,128)(2,1)}) %all-gather.10.cloned.1.call-update) | async-done | bytes 2359312 | tf_op jit(solution)/shard_map/all_gather | solution.py:77
  623.6 4.4 copy.48
  628.0 2.6 fusion.52
  631.5 292.6 %all-gather.8.cloned.1.call-done = bf16[1536,768]{1,0:T(8,128)(2,1)} async-done(((bf16[24,768]{1,0:T(8,128)(2,1)}), bf16[1536,768]{1,0:T(8,128)(2,1)}) %all-gather.8.cloned.1.call-update) | async-done | bytes 2359312 | tf_op jit(solution)/shard_map/all_gather | solution.py:78
  924.0 2.5 convolution_convert_fusion.1
  928.3 1.7 maximum_bitcast_fusion.1
  930.0 26.4 %all-gather.14.cloned.1.call-done = bf16[1024,1536]{0,1:T(8,128)(2,1)} async-done(((bf16[256,1536]{0,1:T(8,128)(2,1)}), bf16[1024,1536]{0,1:T(8,128)(2,1)}) %all-gather.14.cloned.1.call-update) | async-done | bytes 3145744 | tf_op jit(solution)/shard_map/all_gather | solution.py:87
  956.4 69.6 %while.14 = (s32[]{:T(128)}, bf16[8,1024,2,96]{1,3,2,0:T(8,128)(2,1)}, f32[8,2,1024]{2,1,0:T(2,128)}, f32[8,2,1024]{2,1,0:T(2,128)}, bf16[8,768,96]{1,2,0:T(8,12...) while((s32[]{:T(128)}, ...), condition=%wide.region_4.5_spmd, body=%wide.region_1.4_spmd.sunk | while | flops 624818176 | bytes 22407772 | solution.py:124
  956.4 2.5 fusion.68
  959.0 1.7 fusion.69
  961.2 3.9 fusion.70
  965.1 2.6 fusion.68
  967.7 1.7 fusion.69
  970.0 3.9 fusion.70
  973.8 2.5 fusion.68
  976.4 1.7 fusion.69
  978.7 3.9 fusion.70
  982.6 2.6 fusion.68
  985.1 1.7 fusion.69
  987.4 3.9 fusion.70
  991.3 2.6 fusion.68
  993.9 1.7 fusion.69
  996.1 3.9 fusion.70
  1000.0 2.6 fusion.68
  1002.6 1.7 fusion.69
  1004.8 3.9 fusion.70
  1008.7 2.5 fusion.68
  1011.2 1.7 fusion.69
  1013.5 3.9 fusion.70
  1017.4 2.6 fusion.68
  1019.9 1.7 fusion.69
  1022.2 3.9 fusion.70
  1026.1 4.8 all_to_all.6
  1030.9 2.0 copy.50
  1032.9 6.9 all-to-all-start
  1042.6 55.7 %all_gather.40 = f32[4,16,1024]{2,1,0:T(8,128)S(1)} all-gather(f32[1,16,1024]{2,1,0:T(8,128)S(1)} %broadcast_in_dim_reshape.6), channel_id=1, replica_groups=mesh['req'=64,'kv'=4] {'kv'}, dimensions={0}, use_global_device_ids=true | all-gather | bytes 327680 | tf_op jit(solution)/shard_map/all_gather | solution.py:129
  1098.2 8.7 all_gather.41
  1107.0 1.5 fusion.43
  1108.6 158.3 %all-gather.16.cloned.1.call-done = bf16[1536,1536]{1,0:T(8,128)(2,1)} async-done(((bf16[24,1536]{1,0:T(8,128)(2,1)}), bf16[1536,1536]{1,0:T(8,128)(2,1)}) %all-gather.16.cloned.1.call-update) | async-done | bytes 4718608 | tf_op jit(solution)/shard_map/all_gather | solution.py:139
  1266.9 4.9 fusion.33
  (78 shorter events, 15.4 us)
Async XLA Ops:
  7.2 316.8 %all-gather.12.cloned.1.call-start = ((), (), s32[]{:S(2)}) async-start(), calls=%async_computation.3 | async-start | bytes 4792320 | tf_op jit(solution)/shard_map/all_gather | solution.py:76
  14.8 608.9 %all-gather.10.cloned.1.call-start = ((), (), s32[]{:S(2)}) async-start(), calls=%async_computation.2 | async-start | bytes 2396160 | tf_op jit(solution)/shard_map/all_gather | solution.py:77
  22.5 901.5 %all-gather.8.cloned.1.call-start = ((), (), s32[]{:S(2)}) async-start(), calls=%async_computation.1 | async-start | bytes 2396160 | tf_op jit(solution)/shard_map/all_gather | solution.py:78
  30.3 926.1 %all-gather.14.cloned.1.call-start = ((), (), s32[]{:S(2)}) async-start(), calls=%async_computation.4 | async-start | bytes 3932160 | tf_op jit(solution)/shard_map/all_gather | solution.py:87
  33.3 301.2 %copy-start.4 = (f32[256,48]{0,1:T(8,128)}, f32[256,48]{0,1:T(8,128)S(1)}, u32[]{:S(2)}) copy-start(f32[256,48]{0,1:T(8,128)S(1)} %get-tuple-element.92) | copy-start | bytes 147460
  33.3 301.2 %copy-start.6 = (f32[256,48]{0,1:T(8,128)}, f32[256,48]{0,1:T(8,128)S(1)}, u32[]{:S(2)}) copy-start(f32[256,48]{0,1:T(8,128)S(1)} %get-tuple-element.93) | copy-start | bytes 147460
  323.9 6.8 copy-start.2
  334.6 1.3 copy-start.9
  334.6 8.9 copy-start
  334.9 8.9 copy-start.1
  335.9 931.0 %all-gather.16.cloned.1.call-start = ((), (), s32[]{:S(2)}) async-start(), calls=%async_computation.5 | async-start | bytes 4792320 | tf_op jit(solution)/shard_map/all_gather | solution.py:139
  623.6 4.4 copy-start.3
  628.0 2.6 copy-start.5
  628.0 2.6 copy-start.7
  926.5 0.7 copy-start.8
  1032.9 74.1 %all-to-all-start = ((bf16[4,256,1536]{1,2,0:T(8,128)(2,1)}), bf16[4,256,1536]{1,2,0:T(8,128)(2,1)S(1)}, u32[]{:S(2)}, u32[]{:S(2)}) async-start(bf16[4,256,1536]{1,2,0:T(8,128)(2,1)} %copy.50), calls=%async_computation | async-start | bytes 6291456 | tf_op jit(solution)/shard_map/all_to_all | solution.py:134
Sparse Core Ops, SparseCore 0:
  14.9 308.9 all-gather.11
  325.7 297.8 all-gather.9
  625.4 298.5 all-gather.7
  926.2 30.1 all-gather.13
  958.1 308.7 all-gather.15
where the time goes:
time: 1280 us
  waiting for transfers between devices  1050 us (82%)
  blocking collectives  93.3 us (7%)
  matrix products  65.2 us (5%)
  local copies, waits for them, and re-layouts  28.3 us (2%)
  other arithmetic  22.5 us (2%)
  between operations  14.7 us (1%)
    all_gather x1, waiting for transfers between devices, body(): lax.all_gather(value_cols, 'req', axis=0, tiled=True)  293 us
    all_gather x1, waiting for transfers between devices, body(): lax.all_gather(query_cols, 'req', axis=0, tiled=True)  291 us
    all_gather x1, waiting for transfers between devices, body(): lax.all_gather(key_cols, 'req', axis=0, tiled=True)  279 us
    all_gather x1, waiting for transfers between devices, body(): lax.all_gather(out_cols, 'req', axis=0, tiled=True)  158 us
    all_gather x1, blocking collectives, body(): lax.all_gather(peaks[None], 'kv', axis=0, tiled=True)  55.7 us
    dot_general x8, matrix products, attend(): jnp.einsum('gqk,kd->qgd', weights.astype(jnp.bfloat16), value_block, pref...  31 us
    all_gather x1, waiting for transfers between devices, body(): queries = lax.all_gather(queries_here, 'kv', axis=0, tiled=True)  26.4 us
  transfers between devices with their start and end apart: 6, of which 5 were waited for; matrix products, arithmetic and copies ran while one was open for 8% of the time, Pallas kernels for 0%

commit v1 on v0

--- a/solution.py
+++ b/solution.py
@@ -1,3 +1,4 @@
+import functools
 import jax
 import jax.numpy as jnp
 from jax import lax
@@ -8,6 +9,19 @@
 HD = 96
 rope_base = 100000.0
 masked_score = -1e30
+
+
+def make_squares(vec, a_name):
+    aux = jnp.concatenate(
+        lax.all_to_all(
+            jnp.stack([vec for _ in range(lax.axis_size(a_name))], axis=0), a_name, 0, 0
+        ),
+        axis=0,
+    )
+    return aux
+
+
+follow_the_desk = functools.partial(make_squares, a_name="req")
 
 
 def rms_norm(states, gain):
@@ -73,7 +87,7 @@
     proj_query, proj_key, proj_value = fold_three(
         normed,
         (
-            lax.all_gather(query_cols, "req", axis=0, tiled=True),
+            follow_the_desk(query_cols),
             lax.all_gather(key_cols, "req", axis=0, tiled=True),
             lax.all_gather(value_cols, "req", axis=0, tiled=True),
         ),

time: 1280 us -> 1010 us (0.79)
  waiting for transfers between devices: 1050 us -> 762 us
  starting transfers between devices: 7.15 us -> 20.1 us
    all_gather x1 -> x0, waiting for transfers between devices: 291 us -> none  [body(): lax.all_gather(query_cols, 'req', axis=0, tiled=True)]
    all_to_all x0 -> x1, waiting for transfers between devices: none -> 93.2 us  [make_squares(): lax.all_to_all(jnp.stack([vec for _ in range(lax.axis_size(a_name))], axi...]
    all_gather x1, waiting for transfers between devices: 279 us -> 190 us  [body(): lax.all_gather(key_cols, 'req', axis=0, tiled=True)]
    all_to_all x0 -> x1, starting transfers between devices: none -> 13 us  [make_squares(): lax.all_to_all(jnp.stack([vec for _ in range(lax.axis_size(a_name))], axi...]
  transfers between devices with their start and end apart: 6 -> 6, of which waited for: 5 -> 5; matrix products, arithmetic and copies ran while one was open for 8% -> 10% of each run, Pallas kernels for 0% -> 0%
where the time goes in v1:
time: 1010 us
  waiting for transfers between devices  762 us (75%)
  blocking collectives  97.8 us (10%)
  matrix products  65.3 us (6%)
  local copies, waits for them, and re-layouts  30.7 us (3%)
  other arithmetic  20.7 us (2%)
  starting transfers between devices  20.1 us (2%)
  between operations  14.8 us (1%)
    all_gather x1, waiting for transfers between devices, body(): lax.all_gather(value_cols, 'req', axis=0, tiled=True)  293 us
    all_gather x1, waiting for transfers between devices, body(): lax.all_gather(key_cols, 'req', axis=0, tiled=True)  190 us
    all_gather x1, waiting for transfers between devices, body(): lax.all_gather(out_cols, 'req', axis=0, tiled=True)  159 us
    all_to_all x1, waiting for transfers between devices, make_squares(): lax.all_to_all(jnp.stack([vec for _ in range(lax.axis_size(a_name))], axi...  93.2 us
    all_gather x1, blocking collectives, body(): lax.all_gather(peaks[None], 'kv', axis=0, tiled=True)  55.6 us
    dot_general x8, matrix products, attend(): jnp.einsum('gqk,kd->qgd', weights.astype(jnp.bfloat16), value_block, pref...  31 us
    all_gather x1, waiting for transfers between devices, body(): queries = lax.all_gather(queries_here, 'kv', axis=0, tiled=True)  26.6 us
    dot_general x8, matrix products, attend(): jnp.einsum('qgd,kd->gqk', query_block, key_block, preferred_element_type=...  20.5 us
  transfers between devices with their start and end apart: 6, of which 5 were waited for; matrix products, arithmetic and copies ran while one was open for 10% of the time, Pallas kernels for 0%

profile of v1, /device:TPU:16, one launch (start us, length us, event | category | flops | bytes accessed | tf_op | source)
XLA Modules:
  0.0 1011.4 jit_solution(17686261308464075647)
XLA Ops:
  7.2 7.0 all_gather.34
  14.2 2.5 stack.2
  16.7 13.0 %all-to-all-start = ((bf16[64,24,1536]{2,1,0:T(8,128)(2,1)}), bf16[64,24,1536]{2,1,0:T(8,128)(2,1)}, u32[]{:S(2)}, u32[]{:S(2)}) async-start(bf16[64,24,1536]{2,1,0:T(8,128)(2,1)} %stack.2), calls=%async_computation | async-start | bytes 9437184 | tf_op jit(solution)/shard_map/all_to_all | solution.py:16
  29.8 12.4 %all-gather.1 = bf16[4,192,24]{1,2,0:T(8,128)(2,1)S(1)} all-gather(bf16[1,192,24]{1,2,0:T(8,128)(2,1)S(1)} %bitcast.199), channel_id=1, replica_groups=mesh['req'=64,'kv'=4] {'kv'}, dimensions={0}, use_global_device_ids=true | all-gather | bytes 46080 | tf_op jit(solution)/shard_map/all_gather | solution.py:84
  43.0 6.8 all-gather
  51.9 93.2 %all-to-all-done = bf16[64,24,1536]{2,1,0:T(8,128)(2,1)} async-done(((bf16[64,24,1536]{2,1,0:T(8,128)(2,1)}), bf16[64,24,1536]{2,1,0:T(8,128)(2,1)}, u32[]{:S(2)}, u32[]{:S(2)}) %all-to-all-start) | async-done | bytes 4718624 | tf_op jit(solution)/shard_map/all_to_all | solution.py:16
  145.1 6.7 copy.49
  151.7 3.9 fusion.50
  156.9 7.5 all_gather.38
  165.7 190.4 %all-gather.9.cloned.1.call-done = bf16[1536,768]{1,0:T(8,128)(2,1)} async-done(((bf16[24,768]{1,0:T(8,128)(2,1)}), bf16[1536,768]{1,0:T(8,128)(2,1)}) %all-gather.9.cloned.1.call-update) | async-done | bytes 2359312 | tf_op jit(solution)/shard_map/all_gather | solution.py:91
  356.1 4.4 copy.48
  360.5 2.6 fusion.52
  363.9 292.9 %all-gather.7.cloned.1.call-done = bf16[1536,768]{1,0:T(8,128)(2,1)} async-done(((bf16[24,768]{1,0:T(8,128)(2,1)}), bf16[1536,768]{1,0:T(8,128)(2,1)}) %all-gather.7.cloned.1.call-update) | async-done | bytes 2359312 | tf_op jit(solution)/shard_map/all_gather | solution.py:92
  656.8 2.5 convolution_convert_fusion.1
  661.1 1.7 maximum_bitcast_fusion.1
  662.8 26.6 %all-gather.11.cloned.1.call-done = bf16[1024,1536]{0,1:T(8,128)(2,1)} async-done(((bf16[256,1536]{0,1:T(8,128)(2,1)}), bf16[1024,1536]{0,1:T(8,128)(2,1)}) %all-gather.11.cloned.1.call-update) | async-done | bytes 3145744 | tf_op jit(solution)/shard_map/all_gather | solution.py:101
  689.4 69.6 %while.14 = (s32[]{:T(128)}, bf16[8,1024,2,96]{1,3,2,0:T(8,128)(2,1)}, f32[8,2,1024]{2,1,0:T(2,128)}, f32[8,2,1024]{2,1,0:T(2,128)}, bf16[8,768,96]{1,2,0:T(8,12...) while((s32[]{:T(128)}, ...), condition=%wide.region_4.5_spmd, body=%wide.region_1.4_spmd.sunk | while | flops 624818176 | bytes 22407772 | solution.py:138
  689.4 2.6 fusion.68
  692.0 1.7 fusion.69
  694.2 3.9 fusion.70
  698.1 2.6 fusion.68
  700.7 1.7 fusion.69
  703.0 3.9 fusion.70
  706.8 2.6 fusion.68
  709.4 1.7 fusion.69
  711.7 3.9 fusion.70
  715.6 2.6 fusion.68
  718.1 1.7 fusion.69
  720.4 3.9 fusion.70
  724.3 2.6 fusion.68
  726.8 1.7 fusion.69
  729.1 3.9 fusion.70
  733.0 2.6 fusion.68
  735.5 1.7 fusion.69
  737.8 3.9 fusion.70
  741.6 2.5 fusion.68
  744.2 1.7 fusion.69
  746.5 3.9 fusion.70
  750.3 2.6 fusion.68
  752.9 1.7 fusion.69
  755.2 3.9 fusion.70
  759.0 4.8 all_to_all.10
  763.9 2.0 copy.50
  765.9 6.9 all-to-all-start.1
  775.5 55.6 %all_gather.36 = f32[4,16,1024]{2,1,0:T(8,128)S(1)} all-gather(f32[1,16,1024]{2,1,0:T(8,128)S(1)} %broadcast_in_dim_reshape.6), channel_id=1, replica_groups=mesh['req'=64,'kv'=4] {'kv'}, dimensions={0}, use_global_device_ids=true | all-gather | bytes 327680 | tf_op jit(solution)/shard_map/all_gather | solution.py:143
  831.1 8.5 all_gather.37
  841.2 158.8 %all-gather.13.cloned.1.call-done = bf16[1536,1536]{1,0:T(8,128)(2,1)} async-done(((bf16[24,1536]{1,0:T(8,128)(2,1)}), bf16[1536,1536]{1,0:T(8,128)(2,1)}) %all-gather.13.cloned.1.call-update) | async-done | bytes 4718608 | tf_op jit(solution)/shard_map/all_gather | solution.py:153
  1000.0 4.9 fusion.33
  (84 shorter events, 16.4 us)
Async XLA Ops:
  16.7 13.1 %copy-start.10 = (bf16[24,192]{1,0:T(8,128)(2,1)S(1)}, bf16[24,192]{1,0:T(8,128)(2,1)}, u32[]{:S(2)}) copy-start(bf16[24,192]{1,0:T(8,128)(2,1)} %param.17) | copy-start | bytes 27652
  16.7 26.4 %copy-start.11 = (bf16[24,192]{1,0:T(8,128)(2,1)S(1)}, bf16[24,192]{1,0:T(8,128)(2,1)}, u32[]{:S(2)}) copy-start(bf16[24,192]{1,0:T(8,128)(2,1)} %param.18) | copy-start | bytes 27652
  16.7 34.6 %copy-start.12 = (bf16[1536]{0:T(1024)(128)(2,1)S(1)}, bf16[1536]{0:T(1024)(128)(2,1)}, u32[]{:S(2)}) copy-start(bf16[1536]{0:T(1024)(128)(2,1)} %param.15) | copy-start | bytes 9220
  16.7 34.7 %copy-start.2 = (bf16[1,256,1536]{2,1,0:T(8,128)(2,1)S(1)}, bf16[1,256,1536]{2,1,0:T(8,128)(2,1)}, u32[]{:S(2)}) copy-start(bf16[1,256,1536]{2,1,0:T(8,128)(2,1)} %param.11) | copy-start | bytes 2359300
  16.7 128.4 %all-to-all-start = ((bf16[64,24,1536]{2,1,0:T(8,128)(2,1)}), bf16[64,24,1536]{2,1,0:T(8,128)(2,1)}, u32[]{:S(2)}, u32[]{:S(2)}) async-start(bf16[64,24,1536]{2,1,0:T(8,128)(2,1)} %stack.2), calls=%async_computation | async-start | bytes 9437184 | tf_op jit(solution)/shard_map/all_to_all | solution.py:16
  29.7 326.4 %all-gather.9.cloned.1.call-start = ((), (), s32[]{:S(2)}) async-start(), calls=%async_computation.3 | async-start | bytes 2396160 | tf_op jit(solution)/shard_map/all_gather | solution.py:91
  43.0 613.9 %all-gather.7.cloned.1.call-start = ((), (), s32[]{:S(2)}) async-start(), calls=%async_computation.2 | async-start | bytes 2396160 | tf_op jit(solution)/shard_map/all_gather | solution.py:92
  50.6 638.8 %all-gather.11.cloned.1.call-start = ((), (), s32[]{:S(2)}) async-start(), calls=%async_computation.4 | async-start | bytes 3932160 | tf_op jit(solution)/shard_map/all_gather | solution.py:101
  51.9 103.7 %copy-start.4 = (f32[256,48]{0,1:T(8,128)}, f32[256,48]{0,1:T(8,128)S(1)}, u32[]{:S(2)}) copy-start(f32[256,48]{0,1:T(8,128)S(1)} %get-tuple-element.92) | copy-start | bytes 147460
  51.9 103.7 %copy-start.6 = (f32[256,48]{0,1:T(8,128)}, f32[256,48]{0,1:T(8,128)S(1)}, u32[]{:S(2)}) copy-start(f32[256,48]{0,1:T(8,128)S(1)} %get-tuple-element.93) | copy-start | bytes 147460
  155.6 1.3 copy-start.9
  155.6 8.9 copy-start
  155.9 8.9 copy-start.1
  156.9 843.1 %all-gather.13.cloned.1.call-start = ((), (), s32[]{:S(2)}) async-start(), calls=%async_computation.5 | async-start | bytes 4792320 | tf_op jit(solution)/shard_map/all_gather | solution.py:153
  356.1 4.4 copy-start.3
  360.4 2.6 copy-start.5
  360.5 2.6 copy-start.7
  659.3 0.7 copy-start.8
  765.9 73.7 %all-to-all-start.1 = ((bf16[4,256,1536]{1,2,0:T(8,128)(2,1)}), bf16[4,256,1536]{1,2,0:T(8,128)(2,1)S(1)}, u32[]{:S(2)}, u32[]{:S(2)}) async-start(bf16[4,256,1536]{1,2,0:T(8,128)(2,1)} %copy.50), calls=%async_computation.1 | async-start | bytes 6291456 | tf_op jit(solution)/shard_map/all_to_all | solution.py:148
Sparse Core Ops, SparseCore 0:
  43.1 312.9 all-gather.8
  357.9 298.9 all-gather.6
  659.2 30.1 all-gather.10
  691.0 308.9 all-gather.12
